TPU v7x, 32 devices: a whole 2x2x4 slice. The times are simulated.
32 devices in a mesh: groups: 2 (over x), seq: 8 (over z, y), head: 2 (over core).
Axes of the slice: x: 2, y: 2, z: 4, core: 2. Of those that a mesh axis runs over, the one named last changes fastest.
Arguments:
- queries: bfloat16 [512, 4096], P(('groups', 'seq'), 'head'), parts along dimension 0, may hold values from -24 to 24
- vision: bfloat16 [4096, 7680], P(('groups', 'seq')), parts along dimension 0, may hold values from -6 to 6
- key_matrix: bfloat16 [7680, 512], P('seq', 'head'), may hold values from -0.0625 to 0.0625
- value_matrix: bfloat16 [7680, 512], P('seq', 'head'), may hold values from -0.0625 to 0.0625
- out_weight: bfloat16 [4096, 8192], P('head', 'seq'), may hold values from -0.09375 to 0.09375
- residual: bfloat16 [512, 8192], P(('groups', 'head'), 'seq'), parts along dimension 0, may hold values from -4 to 4
- query_norm_gain: float32 [128], replicated, may hold values from 1 to 12
- key_norm_gain: float32 [128], replicated, may hold values from 1 to 12
- attn_gate: float32 [1], replicated, may hold values from 0.5 to 2
Outputs:
- mixed: bfloat16 [512, 8192], P(('groups', 'head'), 'seq'), parts along dimension 0
There are 2 independent parts, one for each index of `groups`. A program takes and returns all parts, laid end to end along the dimension named above; an argument that names none is the same for every part. Nothing has to cross between parts.
All inputs are finite; a program needn't handle non-finite values.
Results may differ from a plain program's by a relative error of at most 0.015.
The roundings to bfloat16 on the way count: a program that leaves them out, or rounds other values in their place, can miss the bound.
Values may be sent and summed in bfloat16 or wider, within the bound.
A program may use at most 64 MiB of HBM per device.

v0:
```python
import jax
import jax.numpy as jnp
from jax import lax
from jax.sharding import PartitionSpec as P

HEAD_SIZE = 128
epsilon = 1e-05


def apply_norm(value_heads, gain):
    return (
        value_heads
        * lax.rsqrt(jnp.mean(value_heads * value_heads, axis=-1, keepdims=True) + epsilon)
        * gain
    )


def body(
    queries,
    vision,
    key_matrix,
    value_matrix,
    out_weight,
    residual,
    query_norm_gain,
    key_norm_gain,
    attn_gate,
):
    vision_rows = vision.shape[0]
    column_count = key_matrix.shape[1]
    expanded_keys = jnp.dot(
        vision,
        lax.all_gather(key_matrix, "seq", axis=0, tiled=True),
        preferred_element_type=jnp.float32,
    )
    expanded_values = jnp.dot(
        vision,
        lax.all_gather(value_matrix, "seq", axis=0, tiled=True),
        preferred_element_type=jnp.float32,
    )
    kv_local = column_count // HEAD_SIZE
    key_heads = apply_norm(
        expanded_keys.reshape(vision_rows, kv_local, HEAD_SIZE), key_norm_gain
    ).astype(jnp.bfloat16)
    value_heads = expanded_values.reshape(vision_rows, kv_local, HEAD_SIZE).astype(jnp.bfloat16)
    text_rows = queries.shape[0]
    heads_local = queries.shape[1] // HEAD_SIZE
    heads_per_group = heads_local // kv_local
    norm_result = apply_norm(
        queries.astype(jnp.float32).reshape(text_rows, kv_local, heads_per_group, HEAD_SIZE),
        query_norm_gain,
    ).astype(jnp.bfloat16)
    scale = HEAD_SIZE ** (-0.5)
    start_max = jnp.full((text_rows, kv_local, heads_per_group), -1e30, jnp.float32)
    start_den = jnp.zeros((text_rows, kv_local, heads_per_group), jnp.float32)
    start_num = jnp.zeros((text_rows, kv_local, heads_per_group, HEAD_SIZE), jnp.float32)
    key_piece = lax.all_gather(key_heads, "seq", axis=0, tiled=True)
    value_piece = lax.all_gather(value_heads, "seq", axis=0, tiled=True)
    piece_rows = key_piece.shape[0]
    rows_per_block = 512
    key_blocks = key_piece.reshape(
        piece_rows // rows_per_block, rows_per_block, kv_local, HEAD_SIZE
    )
    value_blocks = value_piece.reshape(
        piece_rows // rows_per_block, rows_per_block, kv_local, HEAD_SIZE
    )

    def advance(state_now, both):
        maxima, denominator, numerator = state_now
        scores = (
            jnp.einsum("tgqd,rgd->tgqr", norm_result, both[0], preferred_element_type=jnp.float32)
            * scale
        )
        new_max = jnp.maximum(maxima, jnp.max(scores, axis=-1))
        rescale = jnp.exp(maxima - new_max)
        weights = jnp.exp(scores - new_max[..., None])
        denominator = denominator * rescale + jnp.sum(weights, axis=-1)
        numerator = numerator * rescale[..., None] + jnp.einsum(
            "tgqr,rgd->tgqd",
            weights.astype(jnp.bfloat16),
            both[1],
            preferred_element_type=jnp.float32,
        )
        return ((new_max, denominator, numerator), None)

    maxima, denominator, numerator = lax.scan(
        advance, (start_max, start_den, start_num), (key_blocks, value_blocks)
    )[0]
    attended = (
        (numerator / denominator[..., None])
        .astype(jnp.bfloat16)
        .reshape(text_rows, heads_local * HEAD_SIZE)
    )
    partial_out = jnp.dot(
        lax.all_gather(attended, "seq", axis=0, tiled=True),
        out_weight,
        preferred_element_type=jnp.float32,
    )
    projected = lax.psum_scatter(
        partial_out.astype(jnp.bfloat16), "head", scatter_dimension=0, tiled=True
    ).astype(jnp.float32)
    return (residual.astype(jnp.float32) + jnp.tanh(attn_gate[0]) * projected).astype(jnp.bfloat16)


def solution(mesh):
    in_specs = (
        P(("groups", "seq"), "head"),
        P(("groups", "seq"), None),
        P("seq", "head"),
        P("seq", "head"),
        P("head", "seq"),
        P(("groups", "head"), "seq"),
        P(),
        P(),
        P(),
    )
    out_specs = P(("groups", "head"), "seq")
    return jax.shard_map(body, mesh=mesh, in_specs=in_specs, out_specs=out_specs, check_vma=False)
```

profile of v0, /device:TPU:0, one launch (start us, length us, event | category | flops | bytes accessed | tf_op | source)
XLA Modules:
  0.0 306.7 jit_solution(3217196021253669261)
XLA Ops:
  6.5 0.7 all-gather.6.cloned.1.call-update
  7.3 0.0 all-gather.10.cloned.1.call-start
  7.3 0.7 all-gather.10.cloned.1.call-update
  8.0 0.0 copy-start.2
  8.0 0.0 all-gather.8.cloned.1.call-start
  8.1 73.7 %all-gather.6.cloned.1.call-done = bf16[7680,256]{1,0:T(8,128)(2,1)} async-done(((bf16[960,256]{1,0:T(8,128)(2,1)}), bf16[7680,256]{1,0:T(8,128)(2,1)}) %all-gather.6.cloned.1.call-update) | async-done | bytes 3932176 | tf_op jit(solution)/shard_map/all_gather | solution.py:33
  81.8 5.0 %multiply_reduce_fusion.1 = (f32[256,2]{0,1:T(2,128)S(1)}, f32[256,256]{0,1:T(8,128)S(1)}) fusion(bf16[256,7680]{1,0:T(8,128)(2,1)} %param.12, bf16[7680,256]{1,0:T(8,128)(2,1)} %all-gather.6.cloned.1.call-done), kind=kOutput, calls=%fused_computation.27 | convolution fusion | flops 1006763520 | bytes 8128512 | tf_op jit(solution)/shard_map/dot_general | solution.py:31
  86.7 0.1 copy.23
  86.9 0.8 multiply_convert_fusion.1
  87.7 0.0 all-gather.8.cloned.1.call-update
  87.7 0.0 copy-start.1
  87.7 0.0 copy-start.3
  87.7 0.0 all-gather.12.cloned.1.call-start
  87.8 64.3 %all-gather.10.cloned.1.call-done = bf16[7680,256]{1,0:T(8,128)(2,1)} async-done(((bf16[960,256]{1,0:T(8,128)(2,1)}), bf16[7680,256]{1,0:T(8,128)(2,1)}) %all-gather.10.cloned.1.call-update) | async-done | bytes 3932176 | tf_op jit(solution)/shard_map/all_gather | solution.py:38
  152.1 4.9 %convolution_convert_fusion.1 = bf16[256,256]{0,1:T(8,128)(2,1)S(1)} fusion(bf16[256,7680]{1,0:T(8,128)(2,1)} %param.12, bf16[7680,256]{1,0:T(8,128)(2,1)} %all-gather.10.cloned.1.call-done), kind=kOutput, calls=%fused_computation.20 | convolution fusion | flops 1006698496 | bytes 7995392 | tf_op jit(solution)/shard_map/dot_general | solution.py:36
  157.1 0.7 copy.26
  157.8 0.0 all-gather.12.cloned.1.call-update
  157.8 0.0 all-gather.14.cloned.1.call-start
  158.0 0.2 multiply_reduce_fusion
  158.2 0.1 copy.24
  158.3 0.1 copy.25
  158.4 0.1 multiply_convert_fusion
  158.5 34.7 %all-gather.8.cloned.1.call-done = bf16[2048,2,128]{2,0,1:T(8,128)(2,1)} async-done(((bf16[256,2,128]{2,0,1:T(8,128)(2,1)}), bf16[2048,2,128]{2,0,1:T(8,128)(2,1)}) %all-gather.8.cloned.1.call-update) | async-done | bytes 1048592 | tf_op jit(solution)/shard_map/all_gather | solution.py:57
  193.2 41.0 %all-gather.12.cloned.1.call-done = bf16[2048,2,128]{2,0,1:T(8,128)(2,1)} async-done(((bf16[256,2,128]{2,0,1:T(8,128)(2,1)}), bf16[2048,2,128]{2,0,1:T(8,128)(2,1)}) %all-gather.12.cloned.1.call-update) | async-done | bytes 1048592 | tf_op jit(solution)/shard_map/all_gather | solution.py:58
  234.3 12.4 %while.15 = (s32[]{:T(128)}, f32[32,2,8]{0,2,1:T(8,128)S(1)}, f32[32,2,8]{0,2,1:T(8,128)S(1)}, f32[32,2,8,128]{3,0,2,1:T(8,128)S(1)}, bf16[4,512,2,128]{3,1,0,2:...) while((s32[]{:T(128)}, f32[32,2,8]{0,2,1:T(8,128)S(1)}, ...), condition=%wide.region_5.6_spmd.clone, body=%wide.region_2.5_spmd.clone.sunk | while | flops 135989760 | bytes 4358265 | solution.py:86
  234.3 1.3 fusion.31
  235.6 0.3 fusion.32
  235.9 1.4 fusion.34
  237.4 1.3 fusion.31
  238.7 0.3 fusion.32
  239.0 1.4 fusion.34
  240.5 1.3 fusion.31
  241.8 0.3 fusion.32
  242.1 1.4 fusion.34
  243.6 1.3 fusion.31
  244.9 0.3 fusion.32
  245.3 1.4 fusion.34
  246.7 0.1 divide_convert_fusion
  246.8 0.1 copy.30
  246.9 0.7 copy.38
  247.6 0.0 all-gather.14.cloned.1.call-update
  247.6 0.0 copy-start
  247.6 0.0 reduce-scatter.2.cloned.1.call-start
  247.7 39.1 %all-gather.14.cloned.1.call-done = bf16[256,2048]{1,0:T(8,128)(2,1)} async-done(((bf16[32,2048]{1,0:T(8,128)(2,1)}), bf16[256,2048]{1,0:T(8,128)(2,1)}) %all-gather.14.cloned.1.call-update) | async-done | bytes 1048592 | tf_op jit(solution)/shard_map/all_gather | solution.py:95
  286.7 4.6 %convolution_convert_fusion = bf16[256,1024]{1,0:T(8,128)(2,1)} fusion(bf16[256,2048]{1,0:T(8,128)(2,1)} %all-gather.14.cloned.1.call-done, bf16[2048,1024]{1,0:T(8,128)(2,1)} %param.15), kind=kOutput, calls=%fused_computation.19 | convolution fusion | flops 1074003968 | bytes 5767168 | tf_op jit(solution)/shard_map/dot_general | solution.py:94
  291.3 0.0 reduce-scatter.2.cloned.1.call-update
  292.0 6.1 %reduce-scatter.2.cloned.1.call-done = bf16[128,1024]{1,0:T(8,128)(2,1)} async-done(((bf16[256,1024]{1,0:T(8,128)(2,1)}), bf16[128,1024]{1,0:T(8,128)(2,1)}) %reduce-scatter.2.cloned.1.call-update) | async-done | bytes 262160 | tf_op jit(solution)/shard_map/reduce_scatter | solution.py:99
  298.1 1.7 add_convert_fusion
  (25 shorter events, 0.2 us)
Async XLA Ops:
  6.5 75.2 %all-gather.6.cloned.1.call-start = ((), (), s32[]{:S(2)}) async-start(), calls=%async_computation.1 | async-start | bytes 4423680 | tf_op jit(solution)/shard_map/all_gather | solution.py:33
  7.3 144.9 %all-gather.10.cloned.1.call-start = ((), (), s32[]{:S(2)}) async-start(), calls=%async_computation.3 | async-start | bytes 4423680 | tf_op jit(solution)/shard_map/all_gather | solution.py:38
  8.0 78.9 %copy-start.2 = (f32[128]{0:T(128)S(1)}, f32[128]{0:T(128)}, u32[]{:S(2)}) copy-start(f32[128]{0:T(128)} %param.18) | copy-start | bytes 1540
  8.0 185.2 %all-gather.8.cloned.1.call-start = ((), (), s32[]{:S(2)}) async-start(), calls=%async_computation.2 | async-start | bytes 1179648 | tf_op jit(solution)/shard_map/all_gather | solution.py:57
  87.7 70.2 %copy-start.1 = (bf16[32,2048]{1,0:T(8,128)(2,1)S(1)}, bf16[32,2048]{1,0:T(8,128)(2,1)}, u32[]{:S(2)}) copy-start(bf16[32,2048]{1,0:T(8,128)(2,1)} %param.11) | copy-start | bytes 393220
  87.7 70.6 %copy-start.3 = (f32[128]{0:T(128)S(1)}, f32[128]{0:T(128)}, u32[]{:S(2)}) copy-start(f32[128]{0:T(128)} %param.17) | copy-start | bytes 1540
  87.7 146.5 %all-gather.12.cloned.1.call-start = ((), (), s32[]{:S(2)}) async-start(), calls=%async_computation.4 | async-start | bytes 1179648 | tf_op jit(solution)/shard_map/all_gather | solution.py:58
  157.8 128.9 %all-gather.14.cloned.1.call-start = ((), (), s32[]{:S(2)}) async-start(), calls=%async_computation.5 | async-start | bytes 1179648 | tf_op jit(solution)/shard_map/all_gather | solution.py:95
  247.6 50.5 %copy-start = (bf16[128,1024]{1,0:T(8,128)(2,1)S(1)}, bf16[128,1024]{1,0:T(8,128)(2,1)}, u32[]{:S(2)}) copy-start(bf16[128,1024]{1,0:T(8,128)(2,1)} %param.16) | copy-start | bytes 786436
  247.6 50.5 %reduce-scatter.2.cloned.1.call-start = ((), (), s32[]{:S(2)}) async-start(), calls=%async_computation.6 | async-start | bytes 786432 | tf_op jit(solution)/shard_map/reduce_scatter | solution.py:99
Sparse Core Ops, SparseCore 0:
  9.5 72.2 all-gather.5
  84.0 68.1 all-gather.9
  154.3 38.8 all-gather.7
  195.3 38.9 all-gather.11
  247.7 38.9 all-gather.13
  291.5 6.6 reduce-scatter.1
where the time goes:
time: 307 us
  waiting for transfers between devices  260 us (85%)
  matrix products  25.4 us (8%)
  between operations  14.3 us (5%)
  other arithmetic  4.32 us (1%)
    all_gather x1, waiting for transfers between devices, body(): lax.all_gather(key_matrix, 'seq', axis=0, tiled=True)  73.7 us
    all_gather x1, waiting for transfers between devices, body(): lax.all_gather(value_matrix, 'seq', axis=0, tiled=True)  64.3 us
    all_gather x1, waiting for transfers between devices, body(): value_piece = lax.all_gather(value_heads, 'seq', axis=0, tiled=True)  41 us
    all_gather x1, waiting for transfers between devices, body(): lax.all_gather(attended, 'seq', axis=0, tiled=True)  39.1 us
    all_gather x1, waiting for transfers between devices, body(): key_piece = lax.all_gather(key_heads, 'seq', axis=0, tiled=True)  34.7 us
  transfers between devices with their start and end apart: 6, of which 6 were waited for; matrix products, arithmetic and copies ran while one was open for 4% of the time, Pallas kernels for 0%

commit v1 on v0

--- a/solution.py
+++ b/solution.py
@@ -55,7 +55,12 @@
     start_den = jnp.zeros((text_rows, kv_local, heads_per_group), jnp.float32)
     start_num = jnp.zeros((text_rows, kv_local, heads_per_group, HEAD_SIZE), jnp.float32)
     key_piece = lax.all_gather(key_heads, "seq", axis=0, tiled=True)
-    value_piece = lax.all_gather(value_heads, "seq", axis=0, tiled=True)
+    ring = [value_heads]
+    for hop in range(7):
+        ring.append(lax.ppermute(ring[-1], "seq", [(dev, (dev + 1) % 8) for dev in range(8)]))
+    value_piece = jnp.roll(
+        jnp.concatenate(ring[::-1], axis=0), (lax.axis_index("seq") + 1) * ring[0].shape[0], axis=0
+    )
     piece_rows = key_piece.shape[0]
     rows_per_block = 512
     key_blocks = key_piece.reshape(

time: 307 us -> 284 us (0.925)
  waiting for transfers between devices: 260 us -> 240 us
  matrix products: 25.4 us -> 21.5 us
    ppermute x0 -> x7, waiting for transfers between devices: none -> 48.9 us  [body(): lax.ppermute(ring[-1], 'seq', [(dev, (dev + 1) % 8) for dev in range(8)])]
    all_gather x1 -> x0, waiting for transfers between devices: 41 us -> none  [body(): value_piece = lax.all_gather(value_heads, 'seq', axis=0, tiled=True)]
    all_gather x1, waiting for transfers between devices: 73.7 us -> 36.2 us  [body(): lax.all_gather(key_matrix, 'seq', axis=0, tiled=True)]
    all_gather x1, waiting for transfers between devices: 64.3 us -> 73.7 us  [body(): lax.all_gather(value_matrix, 'seq', axis=0, tiled=True)]
    dot_general x4, matrix products: 5.6 us -> 1.72 us  [advance(): jnp.einsum('tgqr,rgd->tgqd', weights.astype(jnp.bfloat16), both[1], prefe...]
  transfers between devices with their start and end apart: 6 -> 12, of which waited for: 6 -> 11; matrix products, arithmetic and copies ran while one was open for 4% -> 4% of each run, Pallas kernels for 0% -> 0%
where the time goes in v1:
time: 284 us; the launch traced here: 283 us
  waiting for transfers between devices  240 us (85%)
  matrix products  21.5 us (8%)
  between operations  14.1 us (5%)
  other arithmetic  4.29 us (2%)
    all_gather x1, waiting for transfers between devices, body(): lax.all_gather(value_matrix, 'seq', axis=0, tiled=True)  73.7 us
    ppermute x7, waiting for transfers between devices, body(): lax.ppermute(ring[-1], 'seq', [(dev, (dev + 1) % 8) for dev in range(8)])  48.9 us
    all_gather x1, waiting for transfers between devices, body(): lax.all_gather(attended, 'seq', axis=0, tiled=True)  39.1 us
    all_gather x1, waiting for transfers between devices, body(): lax.all_gather(key_matrix, 'seq', axis=0, tiled=True)  36.2 us
    all_gather x1, waiting for transfers between devices, body(): key_piece = lax.all_gather(key_heads, 'seq', axis=0, tiled=True)  34.4 us
    reduce_scatter x1, waiting for transfers between devices, body(): lax.psum_scatter(partial_out.astype(jnp.bfloat16), 'head', scatter_dimens...  6.1 us
  transfers between devices with their start and end apart: 12, of which 11 were waited for; matrix products, arithmetic and copies ran while one was open for 4% of the time, Pallas kernels for 0%

profile of v1, /device:TPU:0, one launch (start us, length us, event | category | flops | bytes accessed | tf_op | source)
XLA Modules:
  0.0 283.5 jit_solution(5833378277156233884)
XLA Ops:
  6.5 0.7 all-gather.9.cloned.1.call-update
  7.3 0.0 all-gather.5.cloned.1.call-start
  7.3 0.7 all-gather.5.cloned.1.call-update
  8.0 0.0 all-gather.7.cloned.1.call-start
  8.1 73.7 %all-gather.9.cloned.1.call-done = bf16[7680,256]{1,0:T(8,128)(2,1)} async-done(((bf16[960,256]{1,0:T(8,128)(2,1)}), bf16[7680,256]{1,0:T(8,128)(2,1)}) %all-gather.9.cloned.1.call-update) | async-done | bytes 3932176 | tf_op jit(solution)/shard_map/all_gather | solution.py:38
  81.8 4.9 %convolution_convert_fusion.1 = bf16[256,256]{0,1:T(8,128)(2,1)S(1)} fusion(bf16[256,7680]{1,0:T(8,128)(2,1)} %param.12, bf16[7680,256]{1,0:T(8,128)(2,1)} %all-gather.9.cloned.1.call-done), kind=kOutput, calls=%fused_computation.20 | convolution fusion | flops 1006698496 | bytes 7995392 | tf_op jit(solution)/shard_map/dot_general | solution.py:36
  86.7 0.1 copy.30
  86.8 0.6 collective-permute-start
  87.5 7.2 %collective-permute-done = bf16[256,2,128]{2,0,1:T(8,128)(2,1)S(1)} collective-permute-done((bf16[256,2,128]{2,0,1:T(8,128)(2,1)S(1)}, bf16[256,2,128]{2,0,1:T(8,128)(2,1)S(1)}, u32[]{:S(2)}, u32[]{:S(2)}) %collective-permute-start) | collective-permute-done | bytes 131104 | tf_op jit(solution)/shard_map/ppermute | solution.py:60
  94.8 0.2 multiply_reduce_fusion
  95.0 0.1 copy.28
  95.0 10.3 %collective-permute-done.1 = bf16[256,2,128]{2,0,1:T(8,128)(2,1)S(1)} collective-permute-done((bf16[256,2,128]{2,0,1:T(8,128)(2,1)S(1)}, bf16[256,2,128]{2,0,1:T(8,128)(2,1)S(1)}, u32[]{:S(2)}, u32[]{:S(2)}) %collective-permute-start.1) | collective-permute-done | bytes 131104 | tf_op jit(solution)/shard_map/ppermute | solution.py:60
  105.3 0.1 copy.29
  105.4 10.5 %collective-permute-done.2 = bf16[256,2,128]{2,0,1:T(8,128)(2,1)S(1)} collective-permute-done((bf16[256,2,128]{2,0,1:T(8,128)(2,1)S(1)}, bf16[256,2,128]{2,0,1:T(8,128)(2,1)S(1)}, u32[]{:S(2)}, u32[]{:S(2)}) %collective-permute-start.2) | collective-permute-done | bytes 131104 | tf_op jit(solution)/shard_map/ppermute | solution.py:60
  115.9 0.1 multiply_convert_fusion
  116.1 7.5 %collective-permute-done.3 = bf16[256,2,128]{2,0,1:T(8,128)(2,1)S(1)} collective-permute-done((bf16[256,2,128]{2,0,1:T(8,128)(2,1)S(1)}, bf16[256,2,128]{2,0,1:T(8,128)(2,1)S(1)}, u32[]{:S(2)}, u32[]{:S(2)}) %collective-permute-start.3) | collective-permute-done | bytes 131104 | tf_op jit(solution)/shard_map/ppermute | solution.py:60
  123.6 36.2 %all-gather.5.cloned.1.call-done = bf16[7680,256]{1,0:T(8,128)(2,1)} async-done(((bf16[960,256]{1,0:T(8,128)(2,1)}), bf16[7680,256]{1,0:T(8,128)(2,1)}) %all-gather.5.cloned.1.call-update) | async-done | bytes 3932176 | tf_op jit(solution)/shard_map/all_gather | solution.py:33
  159.8 5.0 %multiply_reduce_fusion.1 = (f32[256,2]{0,1:T(2,128)S(1)}, f32[256,256]{0,1:T(8,128)S(1)}) fusion(bf16[256,7680]{1,0:T(8,128)(2,1)} %param.12, bf16[7680,256]{1,0:T(8,128)(2,1)} %all-gather.5.cloned.1.call-done), kind=kOutput, calls=%fused_computation.27 | convolution fusion | flops 1006763520 | bytes 8128512 | tf_op jit(solution)/shard_map/dot_general | solution.py:31
  164.7 0.1 copy.27
  164.9 1.1 collective-permute-start.5
  166.0 6.6 %collective-permute-done.5 = bf16[256,2,128]{2,0,1:T(8,128)(2,1)S(1)} collective-permute-done((bf16[256,2,128]{2,0,1:T(8,128)(2,1)S(1)}, bf16[256,2,128]{2,0,1:T(8,128)(2,1)S(1)}, u32[]{:S(2)}, u32[]{:S(2)}) %collective-permute-start.5) | collective-permute-done | bytes 131104 | tf_op jit(solution)/shard_map/ppermute | solution.py:60
  172.6 0.8 multiply_convert_fusion.1
  173.4 0.0 all-gather.7.cloned.1.call-update
  173.4 0.0 all-gather.11.cloned.1.call-start
  173.5 6.8 %collective-permute-done.6 = bf16[256,2,128]{2,0,1:T(8,128)(2,1)S(1)} collective-permute-done((bf16[256,2,128]{2,0,1:T(8,128)(2,1)S(1)}, bf16[256,2,128]{2,0,1:T(8,128)(2,1)S(1)}, u32[]{:S(2)}, u32[]{:S(2)}) %collective-permute-start.6) | collective-permute-done | bytes 131104 | tf_op jit(solution)/shard_map/ppermute | solution.py:60
  180.7 0.1 constant_dynamic-slice_fusion
  180.8 34.4 %all-gather.7.cloned.1.call-done = bf16[2048,2,128]{2,0,1:T(8,128)(2,1)} async-done(((bf16[256,2,128]{2,0,1:T(8,128)(2,1)}), bf16[2048,2,128]{2,0,1:T(8,128)(2,1)}) %all-gather.7.cloned.1.call-update) | async-done | bytes 1048592 | tf_op jit(solution)/shard_map/all_gather | solution.py:57
  215.2 8.5 %while.15 = (s32[]{:T(128)}, f32[32,2,8]{0,2,1:T(8,128)S(1)}, f32[32,2,8]{0,2,1:T(8,128)S(1)}, f32[32,2,8,128]{3,0,2,1:T(8,128)S(1)}, bf16[4,512,2,128]{3,1,0,2:...) while((s32[]{:T(128)}, f32[32,2,8]{0,2,1:T(8,128)S(1)}, ...), condition=%wide.region_5.6_spmd.clone, body=%wide.region_2.5_spmd.clone.sunk | while | flops 135989760 | bytes 4371053 | solution.py:91
  215.2 1.3 fusion.31
  216.5 0.3 fusion.32
  216.9 0.4 fusion.34
  217.3 1.3 fusion.31
  218.7 0.3 fusion.32
  219.0 0.4 fusion.34
  219.5 1.3 fusion.31
  220.8 0.3 fusion.32
  221.2 0.4 fusion.34
  221.6 1.3 fusion.31
  223.0 0.3 fusion.32
  223.3 0.4 fusion.34
  223.8 0.1 divide_convert_fusion
  223.9 0.1 copy.36
  224.0 0.7 copy.44
  224.7 0.0 reduce-scatter.2.cloned.1.call-start
  224.7 39.1 %all-gather.11.cloned.1.call-done = bf16[256,2048]{1,0:T(8,128)(2,1)} async-done(((bf16[32,2048]{1,0:T(8,128)(2,1)}), bf16[256,2048]{1,0:T(8,128)(2,1)}) %all-gather.11.cloned.1.call-update) | async-done | bytes 1048592 | tf_op jit(solution)/shard_map/all_gather | solution.py:100
  263.8 4.6 %convolution_convert_fusion = bf16[256,1024]{1,0:T(8,128)(2,1)} fusion(bf16[256,2048]{1,0:T(8,128)(2,1)} %all-gather.11.cloned.1.call-done, bf16[2048,1024]{1,0:T(8,128)(2,1)} %param.15), kind=kOutput, calls=%fused_computation.19 | convolution fusion | flops 1074003968 | bytes 5767168 | tf_op jit(solution)/shard_map/dot_general | solution.py:99
  269.1 6.1 %reduce-scatter.2.cloned.1.call-done = bf16[128,1024]{1,0:T(8,128)(2,1)} async-done(((bf16[256,1024]{1,0:T(8,128)(2,1)}), bf16[128,1024]{1,0:T(8,128)(2,1)}) %reduce-scatter.2.cloned.1.call-update) | async-done | bytes 262160 | tf_op jit(solution)/shard_map/reduce_scatter | solution.py:104
  275.2 1.7 add_convert_fusion
  (53 shorter events, 0.6 us)
Async XLA Ops:
  6.5 75.2 %all-gather.9.cloned.1.call-start = ((), (), s32[]{:S(2)}) async-start(), calls=%async_computation.3 | async-start | bytes 4423680 | tf_op jit(solution)/shard_map/all_gather | solution.py:38
  7.3 152.5 %all-gather.5.cloned.1.call-start = ((), (), s32[]{:S(2)}) async-start(), calls=%async_computation.1 | async-start | bytes 4423680 | tf_op jit(solution)/shard_map/all_gather | solution.py:33
  8.0 86.7 %copy-start.1 = (bf16[32,2048]{1,0:T(8,128)(2,1)S(1)}, bf16[32,2048]{1,0:T(8,128)(2,1)}, u32[]{:S(2)}) copy-start(bf16[32,2048]{1,0:T(8,128)(2,1)} %param.11) | copy-start | bytes 393220
  8.0 107.9 %copy-start.2 = (f32[128]{0:T(128)S(1)}, f32[128]{0:T(128)}, u32[]{:S(2)}) copy-start(f32[128]{0:T(128)} %param.17) | copy-start | bytes 1540
  8.0 207.2 %all-gather.7.cloned.1.call-start = ((), (), s32[]{:S(2)}) async-start(), calls=%async_computation.2 | async-start | bytes 1179648 | tf_op jit(solution)/shard_map/all_gather | solution.py:57
  86.8 7.8 %collective-permute-start = (bf16[256,2,128]{2,0,1:T(8,128)(2,1)S(1)}, bf16[256,2,128]{2,0,1:T(8,128)(2,1)S(1)}, u32[]{:S(2)}, u32[]{:S(2)}) collective-permute-start(bf16[256,2,128]{2,0,1:T(8,128)(2,1)S(1)} %copy.30), channel_id=1, source_target_pairs={{0,2},{2,4},{4,6},{6,8},{8,10},{10,12},{12,14},{14,0},{1,3},{3,5},... | collective-permute-start | bytes 393224 | tf_op jit(solution)/shard_map/ppermute | solution.py:60
  94.7 10.7 %collective-permute-start.1 = (bf16[256,2,128]{2,0,1:T(8,128)(2,1)S(1)}, bf16[256,2,128]{2,0,1:T(8,128)(2,1)S(1)}, u32[]{:S(2)}, u32[]{:S(2)}) collective-permute-start(bf16[256,2,128]{2,0,1:T(8,128)(2,1)S(1)} %collective-permute-done), channel_id=1, source_target_pairs={{0,2},{2,4},{4,6},{6,8},{8,10},{10,12},{12,14},{14,0},{1,3},{3,5},... | collective-permute-start | bytes 393224 | tf_op jit(solution)/shard_map/ppermute | solution.py:60
  105.3 10.6 %collective-permute-start.2 = (bf16[256,2,128]{2,0,1:T(8,128)(2,1)S(1)}, bf16[256,2,128]{2,0,1:T(8,128)(2,1)S(1)}, u32[]{:S(2)}, u32[]{:S(2)}) collective-permute-start(bf16[256,2,128]{2,0,1:T(8,128)(2,1)S(1)} %collective-permute-done.1), channel_id=1, source_target_pairs={{0,2},{2,4},{4,6},{6,8},{8,10},{10,12},{12,14},{14,0},{1,3},{3,5},... | collective-permute-start | bytes 393224 | tf_op jit(solution)/shard_map/ppermute | solution.py:60
  115.9 7.7 %collective-permute-start.3 = (bf16[256,2,128]{2,0,1:T(8,128)(2,1)S(1)}, bf16[256,2,128]{2,0,1:T(8,128)(2,1)S(1)}, u32[]{:S(2)}, u32[]{:S(2)}) collective-permute-start(bf16[256,2,128]{2,0,1:T(8,128)(2,1)S(1)} %collective-permute-done.2), channel_id=1, source_target_pairs={{0,2},{2,4},{4,6},{6,8},{8,10},{10,12},{12,14},{14,0},{1,3},{3,5},... | collective-permute-start | bytes 393224 | tf_op jit(solution)/shard_map/ppermute | solution.py:60
  116.1 56.5 %copy-start.3 = (f32[128]{0:T(128)S(1)}, f32[128]{0:T(128)}, u32[]{:S(2)}) copy-start(f32[128]{0:T(128)} %param.18) | copy-start | bytes 1540
  123.6 41.3 %collective-permute-start.4 = (bf16[256,2,128]{2,0,1:T(8,128)(2,1)S(1)}, bf16[256,2,128]{2,0,1:T(8,128)(2,1)S(1)}, u32[]{:S(2)}, u32[]{:S(2)}) collective-permute-start(bf16[256,2,128]{2,0,1:T(8,128)(2,1)S(1)} %collective-permute-done.3), channel_id=1, source_target_pairs={{0,2},{2,4},{4,6},{6,8},{8,10},{10,12},{12,14},{14,0},{1,3},{3,5},... | collective-permute-start | bytes 393224 | tf_op jit(solution)/shard_map/ppermute | solution.py:60
  164.9 7.7 %collective-permute-start.5 = (bf16[256,2,128]{2,0,1:T(8,128)(2,1)S(1)}, bf16[256,2,128]{2,0,1:T(8,128)(2,1)S(1)}, u32[]{:S(2)}, u32[]{:S(2)}) collective-permute-start(bf16[256,2,128]{2,0,1:T(8,128)(2,1)S(1)} %collective-permute-done.4), channel_id=1, source_target_pairs={{0,2},{2,4},{4,6},{6,8},{8,10},{10,12},{12,14},{14,0},{1,3},{3,5},... | collective-permute-start | bytes 393224 | tf_op jit(solution)/shard_map/ppermute | solution.py:60
  172.6 7.7 %collective-permute-start.6 = (bf16[256,2,128]{2,0,1:T(8,128)(2,1)S(1)}, bf16[256,2,128]{2,0,1:T(8,128)(2,1)S(1)}, u32[]{:S(2)}, u32[]{:S(2)}) collective-permute-start(bf16[256,2,128]{2,0,1:T(8,128)(2,1)S(1)} %collective-permute-done.5), channel_id=1, source_target_pairs={{0,2},{2,4},{4,6},{6,8},{8,10},{10,12},{12,14},{14,0},{1,3},{3,5},... | collective-permute-start | bytes 393224 | tf_op jit(solution)/shard_map/ppermute | solution.py:60
  173.4 90.4 %all-gather.11.cloned.1.call-start = ((), (), s32[]{:S(2)}) async-start(), calls=%async_computation.4 | async-start | bytes 1179648 | tf_op jit(solution)/shard_map/all_gather | solution.py:100
  224.7 50.5 %copy-start = (bf16[128,1024]{1,0:T(8,128)(2,1)S(1)}, bf16[128,1024]{1,0:T(8,128)(2,1)}, u32[]{:S(2)}) copy-start(bf16[128,1024]{1,0:T(8,128)(2,1)} %param.16) | copy-start | bytes 786436
  224.7 50.5 %reduce-scatter.2.cloned.1.call-start = ((), (), s32[]{:S(2)}) async-start(), calls=%async_computation.5 | async-start | bytes 786432 | tf_op jit(solution)/shard_map/reduce_scatter | solution.py:104
Sparse Core Ops, SparseCore 0:
  9.5 72.2 all-gather.8
  84.0 75.7 all-gather.4
  173.5 41.6 all-gather.6
  224.8 38.9 all-gather.10
  268.5 6.6 reduce-scatter.1
